TPU v7x, 32 devices: a whole 2x2x4 slice. The times are simulated.
32 devices in a mesh: tm: 4 (over y, core), chan: 8 (over z, x).
Axes of the slice: x: 2, y: 2, z: 4, core: 2. Of those that a mesh axis runs over, the one named last changes fastest.
Arguments:
- traces: bfloat16 [8, 1024, 1024], P('tm', 'chan'), may hold values from -6 to 6
- lengths: int32 [8], replicated, may hold values from 512 to 1024
- source_blocks: int32 [3], replicated, may hold values from 0 to 31
Outputs:
- stacks: float32 [32, 3, 201, 1024], P('tm', None, None, 'chan')
Inputs may be any that keep to these rules, and one draw needn't show every extreme that they name: Step s takes the source channels 32 * source_blocks[s] to 32 * source_blocks[s] + 31. `lengths`: samples at and after a segment's length are not used.
All inputs are finite; a program needn't handle non-finite values.
Results may differ from a plain program's by a relative error of at most 0.0085.
Values may be sent and summed in bfloat16 or wider, within the bound.
No kernel may reach another device: no remote copies, remote signals or barrier semaphores. Data moves between devices by JAX's collectives and lax.ppermute only.
A program may use at most 256 MiB of HBM per device.

v0:
```python
import jax
import jax.numpy as jnp
from jax import lax
from jax.sharding import PartitionSpec as P

MAXLAG = 100
SRC = 32
epsilon = 1e-06


def whiten(traces, lengths):
    sample_len = traces.shape[2]
    positions = lax.broadcasted_iota(jnp.int32, (1, 1, sample_len), 2)
    valid_mask = (positions < lengths[:, None, None]).astype(jnp.float32)
    masked = traces.astype(jnp.float32) * valid_mask
    seg_count = lengths.astype(jnp.float32)[:, None, None]
    mean_power = jnp.sum(masked * masked, axis=2, keepdims=True) / seg_count
    return (masked / jnp.sqrt(mean_power + epsilon)).astype(jnp.bfloat16)


def correlate(sources, receivers, lengths):
    sample_len = sources.shape[2]
    padded = jnp.pad(sources, ((0, 0), (0, 0), (MAXLAG, MAXLAG)))
    root_count = jnp.sqrt(lengths.astype(jnp.float32))
    lag_total = 2 * MAXLAG + 1
    lag_blocks = []
    for start_lag in range(0, lag_total, 67):
        lag_width = min(67, lag_total - start_lag)
        offsets = start_lag + jnp.arange(lag_width, dtype=jnp.int32)

        def take_lag(lag_value):
            return lax.dynamic_slice_in_dim(padded, 2 * MAXLAG - lag_value, sample_len, 2)

        shifted = jax.vmap(take_lag, out_axes=2)(offsets)
        product = jnp.einsum(
            "gnau,gcu->gnac", shifted, receivers, preferred_element_type=jnp.float32
        )
        lag_blocks.append(jnp.sum(product / root_count[:, None, None, None], axis=0))
    return jnp.concatenate(lag_blocks, axis=1)


def shards(traces, lengths, source_blocks):
    seg_dev = traces.shape[0]
    own_lengths = lax.dynamic_slice_in_dim(lengths, lax.axis_index("tm") * seg_dev, seg_dev, 0)
    whitened = whiten(traces, own_lengths)
    per_owner = whitened.shape[1] // SRC
    step_count = source_blocks.shape[0]
    sources = []
    my_index = lax.axis_index("chan")
    contributions = []
    for step_index in range(step_count):
        owner_index = source_blocks[step_index] // per_owner
        local_start = source_blocks[step_index] % per_owner * SRC
        block_here = lax.dynamic_slice_in_dim(whitened, local_start, SRC, 1).astype(jnp.float32)
        contributions.append(
            jnp.where(owner_index == my_index, block_here, jnp.zeros_like(block_here))
        )
    summed = lax.psum(jnp.stack(contributions), "chan")
    sources = [summed[step_index].astype(jnp.bfloat16) for step_index in range(step_count)]
    results = []
    for step_index in range(step_count):
        chosen = sources[step_index]
        results.append(
            lax.psum_scatter(
                correlate(chosen, whitened, own_lengths).astype(jnp.bfloat16),
                "tm",
                scatter_dimension=0,
                tiled=True,
            ).astype(jnp.float32)
        )
    return jnp.stack(results, axis=1)


def solution(mesh):
    return jax.shard_map(
        shards,
        mesh=mesh,
        in_specs=(P("tm", "chan", None), P(), P()),
        out_specs=P("tm", None, None, "chan"),
        check_vma=False,
    )
```

profile of v0, /device:TPU:0, one launch (start us, length us, event | category | flops | bytes accessed | tf_op | source)
XLA Modules:
  0.0 1519.1 jit_solution(4298698127265527890)
XLA Ops:
  19.2 47.3 %all-reduce.14 = bf16[3,2,32,1024]{3,2,1,0:T(8,128)(2,1)S(1)} all-reduce(f32[3,2,32,1024]{3,2,1,0:T(8,128)S(1)} %pad_maximum_fusion.3), channel_id=1, replica_groups=mesh['tm'=4,'chan'=8] {'chan'}, use_global_device_ids=true, to_apply=%region_1.2 | all-reduce | flops 196608 | bytes 1179648 | tf_op jit(solution)/shard_map/psum | solution.py:58
  66.7 4.5 broadcast.153.clone
  71.2 128.9 %while.9 = (s32[]{:T(128)}, bf16[2,32,1224]{2,1,0:T(8,128)(2,1)S(1)}, s32[67,3]{0,1:T(4,128)S(1)}, bf16[67,2,32,1024]{3,2,1,0:T(8,128)(2,1)}, s32[]{:T(128)}) while((s32[]{:T(128)}, bf16[2,32,1224]{2,1,0:T(8,128)(2,1)S(1)}, s32[67,3]{0,1:T(4,128)S(1)}, bf16[67,2,32,1024]{3,2,1,0:T(8,128)(2,1)}, s32[]{:T(128)}) %tuple.120), condition=%wide.while_cond, body=%wide.while_body.sunk | while | flops 2 | bytes 262765 | solution.py:32
  200.1 5.9 fusion.16
  206.1 4.5 broadcast.153.clone.1
  210.5 133.6 %while.10 = (s32[]{:T(128)}, bf16[2,32,1224]{2,1,0:T(8,128)(2,1)S(1)}, s32[67,3]{0,1:T(4,128)S(1)}, bf16[67,2,32,1024]{3,2,1,0:T(8,128)(2,1)}, s32[]{:T(128)}) while((s32[]{:T(128)}, bf16[2,32,1224]{2,1,0:T(8,128)(2,1)S(1)}, s32[67,3]{0,1:T(4,128)S(1)}, bf16[67,2,32,1024]{3,2,1,0:T(8,128)(2,1)}, s32[]{:T(128)}) %tuple.150), condition=%wide.while_cond.1, body=%wide.while_body.1.sunk | while | flops 2 | bytes 262765 | solution.py:32
  344.1 7.3 fusion.14
  355.9 134.0 %while.11 = (s32[]{:T(128)}, bf16[2,32,1224]{2,1,0:T(8,128)(2,1)S(1)}, s32[67,3]{0,1:T(4,128)S(1)}, bf16[67,2,32,1024]{3,2,1,0:T(8,128)(2,1)}, s32[]{:T(128)}) while((s32[]{:T(128)}, bf16[2,32,1224]{2,1,0:T(8,128)(2,1)S(1)}, s32[67,3]{0,1:T(4,128)S(1)}, bf16[67,2,32,1024]{3,2,1,0:T(8,128)(2,1)}, s32[]{:T(128)}) %tuple.151), condition=%wide.while_cond.2, body=%wide.while_body.2.sunk | while | flops 2 | bytes 262765 | solution.py:32
  489.9 7.4 fusion.12
  497.4 4.5 broadcast.153.clone.3
  501.9 128.0 %while.12 = (s32[]{:T(128)}, bf16[2,32,1224]{2,1,0:T(8,128)(2,1)S(1)}, s32[67,3]{0,1:T(4,128)S(1)}, bf16[67,2,32,1024]{3,2,1,0:T(8,128)(2,1)}, s32[]{:T(128)}) while((s32[]{:T(128)}, bf16[2,32,1224]{2,1,0:T(8,128)(2,1)S(1)}, s32[67,3]{0,1:T(4,128)S(1)}, bf16[67,2,32,1024]{3,2,1,0:T(8,128)(2,1)}, s32[]{:T(128)}) %tuple.156), condition=%wide.while_cond.3, body=%wide.while_body.3.sunk | while | flops 2 | bytes 262765 | solution.py:32
  629.8 7.3 fusion.10
  641.7 141.5 %while.13 = (s32[]{:T(128)}, bf16[2,32,1224]{2,1,0:T(8,128)(2,1)S(1)}, s32[67,3]{0,1:T(4,128)S(1)}, bf16[67,2,32,1024]{3,2,1,0:T(8,128)(2,1)}, s32[]{:T(128)}) while((s32[]{:T(128)}, bf16[2,32,1224]{2,1,0:T(8,128)(2,1)S(1)}, s32[67,3]{0,1:T(4,128)S(1)}, bf16[67,2,32,1024]{3,2,1,0:T(8,128)(2,1)}, s32[]{:T(128)}) %tuple.158), condition=%wide.while_cond.4, body=%wide.while_body.4.sunk | while | flops 2 | bytes 262765 | solution.py:32
  783.1 7.3 fusion.8
  794.9 134.6 %while.14 = (s32[]{:T(128)}, bf16[2,32,1224]{2,1,0:T(8,128)(2,1)S(1)}, s32[67,3]{0,1:T(4,128)S(1)}, bf16[67,2,32,1024]{3,2,1,0:T(8,128)(2,1)}, s32[]{:T(128)}) while((s32[]{:T(128)}, bf16[2,32,1224]{2,1,0:T(8,128)(2,1)S(1)}, s32[67,3]{0,1:T(4,128)S(1)}, bf16[67,2,32,1024]{3,2,1,0:T(8,128)(2,1)}, s32[]{:T(128)}) %tuple.160), condition=%wide.while_cond.5, body=%wide.while_body.5.sunk | while | flops 2 | bytes 262765 | solution.py:32
  929.6 7.3 fusion.6
  941.5 132.3 %while.15 = (s32[]{:T(128)}, bf16[2,32,1224]{2,1,0:T(8,128)(2,1)S(1)}, s32[67,3]{0,1:T(4,128)S(1)}, bf16[67,2,32,1024]{3,2,1,0:T(8,128)(2,1)}, s32[]{:T(128)}) while((s32[]{:T(128)}, bf16[2,32,1224]{2,1,0:T(8,128)(2,1)S(1)}, s32[67,3]{0,1:T(4,128)S(1)}, bf16[67,2,32,1024]{3,2,1,0:T(8,128)(2,1)}, s32[]{:T(128)}) %tuple.157), condition=%wide.while_cond.6, body=%wide.while_body.6.sunk | while | flops 2 | bytes 262765 | solution.py:32
  1073.7 7.3 fusion.4
  1085.5 141.9 %while.16 = (s32[]{:T(128)}, bf16[2,32,1224]{2,1,0:T(8,128)(2,1)S(1)}, s32[67,3]{0,1:T(4,128)S(1)}, bf16[67,2,32,1024]{3,2,1,0:T(8,128)(2,1)}, s32[]{:T(128)}) while((s32[]{:T(128)}, bf16[2,32,1224]{2,1,0:T(8,128)(2,1)S(1)}, s32[67,3]{0,1:T(4,128)S(1)}, bf16[67,2,32,1024]{3,2,1,0:T(8,128)(2,1)}, s32[]{:T(128)}) %tuple.159), condition=%wide.while_cond.7, body=%wide.while_body.7.sunk | while | flops 2 | bytes 262765 | solution.py:32
  1227.4 7.3 fusion.2
  1239.2 134.3 %while.17 = (s32[]{:T(128)}, bf16[2,32,1224]{2,1,0:T(8,128)(2,1)S(1)}, s32[67,3]{0,1:T(4,128)S(1)}, bf16[67,2,32,1024]{3,2,1,0:T(8,128)(2,1)}, s32[]{:T(128)}) while((s32[]{:T(128)}, bf16[2,32,1224]{2,1,0:T(8,128)(2,1)S(1)}, s32[67,3]{0,1:T(4,128)S(1)}, bf16[67,2,32,1024]{3,2,1,0:T(8,128)(2,1)}, s32[]{:T(128)}) %tuple.161), condition=%wide.while_cond.8, body=%wide.while_body.8.sunk | while | flops 2 | bytes 262765 | solution.py:32
  1373.5 7.5 fusion
  1381.0 21.9 %fusion.26 = (bf16[32,67,128]{2,1,0:T(8,128)(2,1)S(1)}, bf16[32,67,128]{2,1,0:T(8,128)(2,1)S(1)}, bf16[32,67,128]{2,1,0:T(8,128)(2,1)S(1)}, bf16[32,67,128]{2,1,...) fusion(f32[2,32,67,128]{3,1,2,0:T(8,128)S(1)} %fusion.16, ...), kind=kLoop, calls=%fused_computation.53 | loop fusion | flops 7409664 | bytes 24698888 | tf_op jit(solution)/shard_map/reduce_sum | solution.py:38
  1410.6 96.7 %all-reduce.13.cloned.1.call-done = (bf16[32,201,128]{2,0,1:T(8,128)(2,1)}, bf16[32,201,128]{2,0,1:T(8,128)(2,1)}, bf16[32,201,128]{2,0,1:T(8,128)(2,1)}) async-done(((bf16[32,201,128]{2,0,1:T(8,128)(2,1)}, bf16[32,201,128]{2,0,1:T(8,128)(2,1)}, bf16[32,201,128]{2,0,1:T(8,128)(2,1)}), (bf16[32,201,128]{2,0,1:T(8,128)(2,1)}, bf16[32,201,128]{2,0,1:T(8,128)(2,1)}, ...) | async-done | bytes 4939792
  (1852 shorter events, 1251.2 us)
Async XLA Ops:
  6.5 1500.7 %all-reduce.13.cloned.1.call-start = ((), (), s32[]{:S(2)}) async-start(), calls=%async_computation | async-start | bytes 9879552
  1373.5 7.5 copy-start
  1373.5 7.5 copy-start.1
  1405.0 4.2 copy-start.2
Sparse Core Ops, SparseCore 0:
  1409.3 97.8 all-reduce.12
where the time goes:
time: 1530 us; the launch traced here: 1520 us
  local copies, waits for them, and re-layouts  1260 us (82%)
  waiting for transfers between devices  96.7 us (6%)
  matrix products  64.6 us (4%)
  blocking collectives  47.3 us (3%)
  other arithmetic  28.4 us (2%)
  between operations  22.2 us (1%)
    gather x1809, local copies, waits for them, and re-layouts  1210 us
    unnamed x2, waiting for transfers between devices  96.7 us
    dot_general x9, matrix products, correlate(): jnp.einsum('gnau,gcu->gnac', shifted, receivers, preferred_element_type=j...  64.6 us
    psum x1, blocking collectives, shards(): summed = lax.psum(jnp.stack(contributions), 'chan')  47.3 us
    unnamed x16, local copies, waits for them, and re-layouts  41.1 us
  transfers between devices with their start and end apart: 1, of which 1 were waited for; matrix products, arithmetic and copies ran while one was open for 0% of the time, Pallas kernels for 0%

commit v1 on v0

--- a/solution.py
+++ b/solution.py
@@ -55,7 +55,7 @@
         contributions.append(
             jnp.where(owner_index == my_index, block_here, jnp.zeros_like(block_here))
         )
-    summed = lax.psum(jnp.stack(contributions), "chan")
+    summed = jnp.sum(lax.all_gather(jnp.stack(contributions), "chan"), axis=0)
     sources = [summed[step_index].astype(jnp.bfloat16) for step_index in range(step_count)]
     results = []
     for step_index in range(step_count):

time: 1530 us -> 1600 us (1.046)
  waiting for transfers between devices: 96.7 us -> 196 us
  blocking collectives: 47.3 us -> 0 us
    all_gather x0 -> x1, waiting for transfers between devices: none -> 101 us  [shards(): summed = jnp.sum(lax.all_gather(jnp.stack(contributions), 'chan'), axis=0)]
    psum x1 -> x0, blocking collectives: 47.3 us -> none  [shards(): summed = lax.psum(jnp.stack(contributions), 'chan')]
    unnamed x2 -> x3, waiting for transfers between devices: 96.7 us -> 94.7 us
  transfers between devices with their start and end apart: 1 -> 2, of which waited for: 1 -> 2; matrix products, arithmetic and copies ran while one was open for 0% -> 0% of each run, Pallas kernels for 0% -> 0%
where the time goes in v1:
time: 1600 us; the launch traced here: 1580 us
  local copies, waits for them, and re-layouts  1260 us (79%)
  waiting for transfers between devices  196 us (12%)
  matrix products  64.7 us (4%)
  other arithmetic  32.8 us (2%)
  between operations  22.3 us (1%)
    gather x1809, local copies, waits for them, and re-layouts  1210 us
    all_gather x1, waiting for transfers between devices, shards(): summed = jnp.sum(lax.all_gather(jnp.stack(contributions), 'chan'), axis=0)  101 us
    unnamed x3, waiting for transfers between devices  94.7 us
    dot_general x9, matrix products, correlate(): jnp.einsum('gnau,gcu->gnac', shifted, receivers, preferred_element_type=j...  64.7 us
    unnamed x16, local copies, waits for them, and re-layouts  41.1 us
  transfers between devices with their start and end apart: 2, of which 2 were waited for; matrix products, arithmetic and copies ran while one was open for 0% of the time, Pallas kernels for 0%

profile of v1, /device:TPU:0, one launch (start us, length us, event | category | flops | bytes accessed | tf_op | source)
XLA Modules:
  0.0 1580.3 jit_solution(1712596574960141180)
XLA Ops:
  20.2 101.4 %all-gather.3.cloned.1.call-done = f32[24,2,32,1024]{3,2,1,0:T(8,128)} async-done(((f32[3,2,32,1024]{3,2,1,0:T(8,128)}), f32[24,2,32,1024]{3,2,1,0:T(8,128)}) %all-gather.3.cloned.1.call-update) | async-done | bytes 6291472 | tf_op jit(solution)/shard_map/all_gather | solution.py:58
  125.3 4.5 broadcast.153.clone
  129.8 133.6 %while.9 = (s32[]{:T(128)}, bf16[2,32,1224]{2,1,0:T(8,128)(2,1)S(1)}, s32[67,3]{0,1:T(4,128)S(1)}, bf16[67,2,32,1024]{3,2,1,0:T(8,128)(2,1)}, s32[]{:T(128)}) while((s32[]{:T(128)}, bf16[2,32,1224]{2,1,0:T(8,128)(2,1)S(1)}, s32[67,3]{0,1:T(4,128)S(1)}, bf16[67,2,32,1024]{3,2,1,0:T(8,128)(2,1)}, s32[]{:T(128)}) %tuple.120), condition=%wide.while_cond, body=%wide.while_body.sunk | while | flops 2 | bytes 262765 | solution.py:32
  263.4 5.9 fusion.16
  269.3 4.5 broadcast.153.clone.1
  273.8 133.6 %while.10 = (s32[]{:T(128)}, bf16[2,32,1224]{2,1,0:T(8,128)(2,1)S(1)}, s32[67,3]{0,1:T(4,128)S(1)}, bf16[67,2,32,1024]{3,2,1,0:T(8,128)(2,1)}, s32[]{:T(128)}) while((s32[]{:T(128)}, bf16[2,32,1224]{2,1,0:T(8,128)(2,1)S(1)}, s32[67,3]{0,1:T(4,128)S(1)}, bf16[67,2,32,1024]{3,2,1,0:T(8,128)(2,1)}, s32[]{:T(128)}) %tuple.154), condition=%wide.while_cond.1, body=%wide.while_body.1.sunk | while | flops 2 | bytes 262765 | solution.py:32
  407.4 7.3 fusion.14
  419.2 134.0 %while.11 = (s32[]{:T(128)}, bf16[2,32,1224]{2,1,0:T(8,128)(2,1)S(1)}, s32[67,3]{0,1:T(4,128)S(1)}, bf16[67,2,32,1024]{3,2,1,0:T(8,128)(2,1)}, s32[]{:T(128)}) while((s32[]{:T(128)}, bf16[2,32,1224]{2,1,0:T(8,128)(2,1)S(1)}, s32[67,3]{0,1:T(4,128)S(1)}, bf16[67,2,32,1024]{3,2,1,0:T(8,128)(2,1)}, s32[]{:T(128)}) %tuple.155), condition=%wide.while_cond.2, body=%wide.while_body.2.sunk | while | flops 2 | bytes 262765 | solution.py:32
  553.1 7.4 fusion.12
  560.6 4.5 broadcast.153.clone.3
  565.1 128.0 %while.12 = (s32[]{:T(128)}, bf16[2,32,1224]{2,1,0:T(8,128)(2,1)S(1)}, s32[67,3]{0,1:T(4,128)S(1)}, bf16[67,2,32,1024]{3,2,1,0:T(8,128)(2,1)}, s32[]{:T(128)}) while((s32[]{:T(128)}, bf16[2,32,1224]{2,1,0:T(8,128)(2,1)S(1)}, s32[67,3]{0,1:T(4,128)S(1)}, bf16[67,2,32,1024]{3,2,1,0:T(8,128)(2,1)}, s32[]{:T(128)}) %tuple.162), condition=%wide.while_cond.3, body=%wide.while_body.3.sunk | while | flops 2 | bytes 262765 | solution.py:32
  693.1 7.3 fusion.10
  704.9 141.5 %while.13 = (s32[]{:T(128)}, bf16[2,32,1224]{2,1,0:T(8,128)(2,1)S(1)}, s32[67,3]{0,1:T(4,128)S(1)}, bf16[67,2,32,1024]{3,2,1,0:T(8,128)(2,1)}, s32[]{:T(128)}) while((s32[]{:T(128)}, bf16[2,32,1224]{2,1,0:T(8,128)(2,1)S(1)}, s32[67,3]{0,1:T(4,128)S(1)}, bf16[67,2,32,1024]{3,2,1,0:T(8,128)(2,1)}, s32[]{:T(128)}) %tuple.160), condition=%wide.while_cond.4, body=%wide.while_body.4.sunk | while | flops 2 | bytes 262765 | solution.py:32
  846.4 7.3 fusion.8
  858.2 134.6 %while.14 = (s32[]{:T(128)}, bf16[2,32,1224]{2,1,0:T(8,128)(2,1)S(1)}, s32[67,3]{0,1:T(4,128)S(1)}, bf16[67,2,32,1024]{3,2,1,0:T(8,128)(2,1)}, s32[]{:T(128)}) while((s32[]{:T(128)}, bf16[2,32,1224]{2,1,0:T(8,128)(2,1)S(1)}, s32[67,3]{0,1:T(4,128)S(1)}, bf16[67,2,32,1024]{3,2,1,0:T(8,128)(2,1)}, s32[]{:T(128)}) %tuple.158), condition=%wide.while_cond.5, body=%wide.while_body.5.sunk | while | flops 2 | bytes 262765 | solution.py:32
  992.8 7.3 fusion.6
  1004.7 132.3 %while.15 = (s32[]{:T(128)}, bf16[2,32,1224]{2,1,0:T(8,128)(2,1)S(1)}, s32[67,3]{0,1:T(4,128)S(1)}, bf16[67,2,32,1024]{3,2,1,0:T(8,128)(2,1)}, s32[]{:T(128)}) while((s32[]{:T(128)}, bf16[2,32,1224]{2,1,0:T(8,128)(2,1)S(1)}, s32[67,3]{0,1:T(4,128)S(1)}, bf16[67,2,32,1024]{3,2,1,0:T(8,128)(2,1)}, s32[]{:T(128)}) %tuple.163), condition=%wide.while_cond.6, body=%wide.while_body.6.sunk | while | flops 2 | bytes 262765 | solution.py:32
  1137.0 7.3 fusion.4
  1148.8 141.9 %while.16 = (s32[]{:T(128)}, bf16[2,32,1224]{2,1,0:T(8,128)(2,1)S(1)}, s32[67,3]{0,1:T(4,128)S(1)}, bf16[67,2,32,1024]{3,2,1,0:T(8,128)(2,1)}, s32[]{:T(128)}) while((s32[]{:T(128)}, bf16[2,32,1224]{2,1,0:T(8,128)(2,1)S(1)}, s32[67,3]{0,1:T(4,128)S(1)}, bf16[67,2,32,1024]{3,2,1,0:T(8,128)(2,1)}, s32[]{:T(128)}) %tuple.161), condition=%wide.while_cond.7, body=%wide.while_body.7.sunk | while | flops 2 | bytes 262765 | solution.py:32
  1290.6 7.3 fusion.2
  1302.5 134.3 %while.17 = (s32[]{:T(128)}, bf16[2,32,1224]{2,1,0:T(8,128)(2,1)S(1)}, s32[67,3]{0,1:T(4,128)S(1)}, bf16[67,2,32,1024]{3,2,1,0:T(8,128)(2,1)}, s32[]{:T(128)}) while((s32[]{:T(128)}, bf16[2,32,1224]{2,1,0:T(8,128)(2,1)S(1)}, s32[67,3]{0,1:T(4,128)S(1)}, bf16[67,2,32,1024]{3,2,1,0:T(8,128)(2,1)}, s32[]{:T(128)}) %tuple.159), condition=%wide.while_cond.8, body=%wide.while_body.8.sunk | while | flops 2 | bytes 262765 | solution.py:32
  1436.7 7.5 fusion
  1444.2 21.9 %fusion.26 = (bf16[32,67,128]{2,1,0:T(8,128)(2,1)S(1)}, bf16[32,67,128]{2,1,0:T(8,128)(2,1)S(1)}, bf16[32,67,128]{2,1,0:T(8,128)(2,1)S(1)}, bf16[32,67,128]{2,1,...) fusion(f32[2,32,67,128]{3,1,2,0:T(8,128)S(1)} %fusion.16, ...), kind=kLoop, calls=%fused_computation.53 | loop fusion | flops 7409664 | bytes 24698888 | tf_op jit(solution)/shard_map/reduce_sum | solution.py:38
  1473.8 94.7 %all-reduce.12.cloned.1.call-done = (bf16[32,201,128]{2,0,1:T(8,128)(2,1)}, bf16[32,201,128]{2,0,1:T(8,128)(2,1)}, bf16[32,201,128]{2,0,1:T(8,128)(2,1)}) async-done(((bf16[32,201,128]{2,0,1:T(8,128)(2,1)}, bf16[32,201,128]{2,0,1:T(8,128)(2,1)}, bf16[32,201,128]{2,0,1:T(8,128)(2,1)}), (bf16[32,201,128]{2,0,1:T(8,128)(2,1)}, bf16[32,201,128]{2,0,1:T(8,128)(2,1)}, ...) | async-done | bytes 4939792
  (1855 shorter events, 1260.3 us)
Async XLA Ops:
  6.5 115.1 %all-gather.3.cloned.1.call-start = ((), (), s32[]{:S(2)}) async-start(), calls=%async_computation | async-start | bytes 7077888 | tf_op jit(solution)/shard_map/all_gather | solution.py:58
  20.1 1548.4 %all-reduce.12.cloned.1.call-start = ((), (), s32[]{:S(2)}) async-start(), calls=%async_computation.1 | async-start | bytes 9879552
  1436.7 7.5 copy-start
  1436.7 7.5 copy-start.1
  1468.2 4.2 copy-start.2
Sparse Core Ops, SparseCore 0:
  20.2 101.3 all-gather.2
  1472.6 95.8 all-reduce.11
